TPU v7x, 128 devices: a whole 4x4x4 slice. The times are simulated.
128 devices in a mesh: dp: 4 (over y), grid: 32 (over z, x, core).
Axes of the slice: x: 4, y: 4, z: 4, core: 2. Of those that a mesh axis runs over, the one named last changes fastest.
Arguments:
- unembed_feature_matrix: bfloat16 [16, 131072, 512], P('dp', 'grid'), may hold values from -6 to 6
- weight_in: bfloat16 [512, 512], replicated, may hold values from -0.25 to 0.25
- bias_in: float32 [512], replicated, may hold values from -3 to 3
- readout_weight: bfloat16 [512], replicated, may hold values from -0.25 to 0.25
- measured_rainfall: float32 [16, 131072], P('dp', 'grid'), may hold values from -20 to 20
- land_mask: int32 [131072], P('grid'), may hold values 0 or 1
- morton: int32 [32, 4096], P('grid'), may hold values from 0 to 4095, each once within a row
Outputs:
- predicted_rainfall: float32 [16, 131072], P('dp', 'grid')
- patch_prediction_deriv: float32 [16, 131072], P('dp', 'grid')
- penalty_per_example: float32 [16], P('dp')
- inner_coefficient_deriv: float32 [512, 512], P('grid')
- offset_projection_derivs: float32 [2, 512], replicated
Inputs may be any that keep to these rules, and one draw needn't show every extreme that they name: `morton`: each row is a permutation of 0 to 4095.
All inputs are finite; a program needn't handle non-finite values. No bound on the sum of `land_mask` on one device may be relied on, other than what follows from the above.
Results may differ from a plain program's by a relative error of at most 0.0029.
Values sent between devices are 32-bit elements; how exact they have to be, the bound alone decides.
No kernel may reach another device: no remote copies, remote signals or barrier semaphores. Data moves between devices by JAX's collectives and lax.ppermute only.
A program may use at most 192 MiB of HBM per device.

v0:
```python
import jax
import jax.numpy as jnp
from jax import lax
from jax.sharding import PartitionSpec as P

sharpness = 0.5


def swapped(block, axis, distance):
    count = lax.axis_size(axis)
    route = []
    for low in range(count):
        high = low | 1 << distance
        if high != low and high < count:
            route += [(low, high), (high, low)]
    return lax.ppermute(block, axis, route)


def smooth_abs(value):
    return jnp.sqrt(1.0 + value * value) - 1.0


def smooth_slope(value):
    return value / jnp.sqrt(1.0 + value * value)


def on_device(
    unembed_feature_matrix, weight_in, bias_in, readout_weight, measured_rainfall, land_mask, morton
):
    example_total, patch_total, width = unembed_feature_matrix.shape
    tiles = lax.axis_size("grid")
    grad_scale = (width / (example_total * lax.axis_size("dp") * patch_total * tiles)) ** 0.5
    flat_rows = unembed_feature_matrix.reshape(example_total * patch_total, width)
    preact = jnp.dot(flat_rows, weight_in, preferred_element_type=jnp.float32) + bias_in
    logistic = jax.nn.sigmoid(preact)
    hidden_activation = (preact * logistic).astype(jnp.bfloat16)
    predicted_rainfall = jnp.dot(
        hidden_activation, readout_weight, preferred_element_type=jnp.float32
    ).reshape(example_total, patch_total)
    patch_penalty_factor = 1.0 + land_mask.astype(jnp.float32)
    prediction_residual = patch_penalty_factor * (predicted_rainfall - measured_rainfall)
    zorder_line = morton[0]
    sorted_entries = jnp.take(prediction_residual, zorder_line, axis=1)
    steepness = jnp.zeros((example_total, patch_total), jnp.float32)
    loss_local = jnp.zeros((example_total,), jnp.float32)
    node_cells = 1
    while node_cells <= patch_total:
        grouped = sorted_entries.reshape(example_total, patch_total // node_cells, node_cells)
        means = jnp.sum(grouped, axis=2) / node_cells
        loss_local = loss_local + node_cells * jnp.sum(smooth_abs(sharpness * means), axis=1)
        steepness = steepness + jnp.repeat(smooth_slope(sharpness * means), node_cells, axis=1)
        node_cells = node_cells * 4
    tile_total = jnp.sum(sorted_entries, axis=1)
    coarse_slope = jnp.zeros((example_total,), jnp.float32)
    bit_count = tiles.bit_length() - 1
    running = tile_total
    for bit_number in range(bit_count):
        running = running + swapped(running, "grid", bit_number)
        if bit_number % 2 == 1 or bit_number == bit_count - 1:
            group = 2 ** (bit_number + 1)
            means = running / (group * patch_total)
            loss_local = loss_local + patch_total * smooth_abs(sharpness * means)
            coarse_slope = coarse_slope + smooth_slope(sharpness * means)
    steepness = steepness + coarse_slope[:, None]
    penalty_per_example = lax.psum(loss_local, "grid") / (patch_total * tiles * sharpness)
    patch_prediction_deriv = (
        jnp.zeros_like(steepness).at[:, zorder_line].set(steepness) * patch_penalty_factor
    )
    derivative_vector = patch_prediction_deriv.reshape(example_total * patch_total)
    epilogue = (
        derivative_vector[:, None]
        * readout_weight.astype(jnp.float32)
        * (logistic * (1.0 + preact * (1.0 - logistic)))
    ).astype(jnp.bfloat16)
    bias_term = jnp.sum(epilogue.astype(jnp.float32), axis=0)
    out_term = jnp.sum(derivative_vector[:, None] * hidden_activation, axis=0)
    vector_term = grad_scale * jnp.stack([bias_term, out_term])
    kept = width // tiles
    weight_term = grad_scale * lax.dot_general(
        flat_rows, epilogue, (((0,), (0,)), ((), ())), preferred_element_type=jnp.float32
    )
    summed, offset_projection_derivs = lax.psum((weight_term, vector_term), ("dp", "grid"))
    inner_coefficient_deriv = lax.dynamic_slice_in_dim(
        summed, lax.axis_index("grid") * kept, kept, 0
    )
    return (
        predicted_rainfall,
        patch_prediction_deriv,
        penalty_per_example,
        inner_coefficient_deriv,
        offset_projection_derivs,
    )


def solution(mesh):
    placed = (P("dp", "grid", None), P(), P(), P(), P("dp", "grid"), P("grid"), P("grid", None))
    return jax.shard_map(
        on_device,
        mesh=mesh,
        in_specs=placed,
        out_specs=(P("dp", "grid"), P("dp", "grid"), P("dp"), P("grid", None), P()),
        check_vma=False,
    )
```

profile of v0, /device:TPU:1, one launch (start us, length us, event | category | flops | bytes accessed | tf_op | source)
XLA Modules:
  0.0 326.8 jit_solution(12811384271982417352)
XLA Ops:
  8.2 29.1 %multiply_convert_fusion.1 = (bf16[16384,512]{1,0:T(8,128)(2,1)}, f32[16384,512]{1,0:T(8,128)}) fusion(f32[512]{0:T(512)} %param.9, bf16[16384,512]{1,0:T(8,128)(2,1)} %bitcast.84, bf16[512,512]{1,0:T(8,128)(2,1)S(1)} %copy-done), kind=kOutput, calls=%fused_computation.5 | convolution fusion | flops 8640266240 | bytes 67635200 | tf_op jit(solution)/shard_map/dot_general | solution.py:34
  37.3 10.2 %fusion.14 = f32[1,16384]{1,0:T(1,128)S(1)} fusion(bf16[16384,512]{1,0:T(8,128)(2,1)} %get-tuple-element.43, bf16[512,1]{0,1:T(2,128)(2,1)S(1)} %reshape.178), kind=kOutput, calls=%fused_computation.73 | convolution fusion | flops 16777216 | bytes 16843776 | tf_op jit(solution)/shard_map/dot_general | solution.py:37
  48.4 2.0 copy.30
  50.4 2.9 subtract_multiply_fusion
  53.3 12.4 %gather_fusion = f32[4096,4]{1,0:T(8,128)S(1)} fusion(f32[4,4096]{0,1:T(8,128)} %subtract_multiply_fusion, s32[4096]{0:T(1024)S(1)} %broadcast_clamp_fusion), kind=kCustom, calls=%fused_computation | custom fusion | bytes 147456 | tf_op jit(solution)/shard_map/jit(_take)/gather | solution.py:43
  65.7 2.3 add_reduce_fusion
  67.9 1.6 collective-permute-start
  69.8 2.2 fusion
  73.8 5.9 %select_reduce_fusion.4 = f32[4,1024]{0,1:T(8,128)S(1)} fusion(f32[4,1024,4]{0,2,1:T(4,128)S(1)} %bitcast.70, pred[1024,4]{1,0:T(8,128)(4,1)S(1)} %compare_and_fusion), kind=kLoop, calls=%fused_computation.23 | loop fusion | flops 28672 | bytes 86016 | tf_op jit(solution)/shard_map/reduce_sum | solution.py:49
  82.9 1.6 select_reduce_fusion.3
  85.0 1.4 collective-permute-start.1
  86.4 1.1 collective-permute-done.1
  87.5 2.9 collective-permute-start.2
  91.4 1.8 collective-permute-start.3
  94.1 3.4 %collective-permute-start.4 = (f32[4]{0:T(128)S(1)}, f32[4]{0:T(128)S(1)}, u32[]{:S(2)}, u32[]{:S(2)}) collective-permute-start(f32[4]{0:T(128)S(1)} %add.245), channel_id=1, source_target_pairs={{0,16},{16,0},{1,17},{17,1},{2,18},{18,2},{3,19},{19,3},{4,20},{20... | collective-permute-start | bytes 56 | tf_op jit(solution)/shard_map/ppermute | solution.py:16
  98.9 3.0 fusion.4
  101.9 11.8 %scatter_custom_fusion = f32[4,4096]{0,1:T(8,128)S(1)} fusion(s32[4096]{0:T(1024)S(1)} %bitcast.81, f32[4,4096]{0,1:T(8,128)} %fusion.4, f32[]{:T(128)} %constant.37.clone.1), kind=kCustom, calls=%fused_computation.9 | custom fusion | bytes 131076 | tf_op jit(solution)/shard_map/scatter | solution.py:67
  113.7 1.9 broadcast_multiply_fusion
  115.6 2.2 copy.38
  117.8 28.0 %convert_reduce_fusion = (f32[512]{0:T(512)S(1)}, bf16[16384,512]{1,0:T(8,128)(2,1)}, f32[512]{0:T(512)S(1)}) fusion(f32[16384,512]{1,0:T(8,128)} %get-tuple-element.44, f32[512]{0:T(512)S(1)} %copy-done.8, f32[512]{0:T(512)S(1)} %convert_element_type.20, f32[16384]{0:T(1024)S(1)} %bitcast.78, bf16[16384,512]{1,0:T(8,128)(2,1)} %get-tuple-element.43), kind=kLoop, calls=%fused_computation.3 | loop fusion | flops 134216704 | bytes 67182592 | tf_op jit(solution)/shard_map/reduce_sum | solution.py:75
  145.8 18.1 %fusion.7 = f32[512,512]{0,1:T(8,128)} fusion(bf16[16384,512]{1,0:T(8,128)(2,1)} %get-tuple-element.28, bf16[16384,512]{1,0:T(8,128)(2,1)} %bitcast.85), kind=kOutput, calls=%fused_computation.30 | convolution fusion | flops 8590196736 | bytes 34603008 | tf_op jit(solution)/shard_map/dot_general | solution.py:79
  164.0 67.4 %psum.21 = f32[4]{0:T(128)S(1)} all-reduce(f32[4]{0:T(128)S(1)} %get-tuple-element.40), channel_id=1, replica_groups=mesh['dp'=4,'grid'=32] {'grid'}, use_global_device_ids=true, to_apply=%region_14.15 | all-reduce | flops 4 | bytes 32 | tf_op jit(solution)/shard_map/psum | solution.py:65
  231.4 64.7 %psum.23 = f32[2,512]{1,0:T(2,128)} all-reduce(f32[2,512]{1,0:T(2,128)S(1)} %maximum_multiply_fusion), channel_id=1, replica_groups=mesh['dp'=4,'grid'=32] {'dp','grid'}, use_global_device_ids=true, to_apply=%region_18.19 | all-reduce | flops 1024 | bytes 8192 | tf_op jit(solution)/shard_map/psum | solution.py:82
  296.6 21.5 %all-reduce.2.cloned.1.call-done = f32[512,512]{0,1:T(8,128)} async-done(((f32[512,512]{0,1:T(8,128)}), f32[512,512]{0,1:T(8,128)}) %all-reduce.2.cloned.1.call-update) | async-done | bytes 1048592 | tf_op jit(solution)/shard_map/psum | solution.py:82
  (69 shorter events, 13.3 us)
Async XLA Ops:
  7.2 1.1 copy-start
  7.2 311.0 %all-reduce.2.cloned.1.call-start = ((), (), s32[]{:S(2)}) async-start(), calls=%async_computation | async-start | bytes 2097152 | tf_op jit(solution)/shard_map/psum | solution.py:82
  37.3 10.2 %copy-start.2 = (s32[1,4096]{1,0:T(1,128)S(1)}, s32[1,4096]{1,0:T(1,128)}, u32[]{:S(2)}) copy-start(s32[1,4096]{1,0:T(1,128)} %param.13) | copy-start | bytes 49156
  47.5 0.9 copy-start.5
  47.6 2.8 copy-start.3
  47.6 2.7 copy-start.6
  65.7 6.3 %copy-start.7 = (bf16[512]{0:T(512)(128)(2,1)S(1)}, bf16[512]{0:T(512)(128)(2,1)}, u32[]{:S(2)}) copy-start(bf16[512]{0:T(512)(128)(2,1)} %param.10) | copy-start | bytes 3076
  67.9 17.0 %collective-permute-start = (f32[4]{0:T(128)S(1)}, f32[4]{0:T(128)S(1)}, u32[]{:S(2)}, u32[]{:S(2)}) collective-permute-start(f32[4]{0:T(128)S(1)} %get-tuple-element.26), channel_id=1, source_target_pairs={{0,1},{1,0},{2,3},{3,2},{4,5},{5,4},{6,7},{7,6},{8,9},{9,8},{10,11... | collective-permute-start | bytes 56 | tf_op jit(solution)/shard_map/ppermute | solution.py:16
  85.0 2.5 collective-permute-start.1
  87.5 3.9 %collective-permute-start.2 = (f32[4]{0:T(128)S(1)}, f32[4]{0:T(128)S(1)}, u32[]{:S(2)}, u32[]{:S(2)}) collective-permute-start(f32[4]{0:T(128)S(1)} %add.242), channel_id=1, source_target_pairs={{0,4},{4,0},{1,5},{5,1},{2,6},{6,2},{3,7},{7,3},{8,12},{12,8},{9,1... | collective-permute-start | bytes 56 | tf_op jit(solution)/shard_map/ppermute | solution.py:16
  91.4 2.7 collective-permute-start.3
  94.1 4.4 %collective-permute-start.4 = (f32[4]{0:T(128)S(1)}, f32[4]{0:T(128)S(1)}, u32[]{:S(2)}, u32[]{:S(2)}) collective-permute-start(f32[4]{0:T(128)S(1)} %add.245), channel_id=1, source_target_pairs={{0,16},{16,0},{1,17},{17,1},{2,18},{18,2},{3,19},{19,3},{4,20},{20... | collective-permute-start | bytes 56 | tf_op jit(solution)/shard_map/ppermute | solution.py:16
  115.6 2.2 copy-start.8
  117.8 28.0 %copy-start.4 = (f32[4,4096]{1,0:T(4,128)}, f32[4,4096]{1,0:T(4,128)S(1)}, u32[]{:S(2)}) copy-start(f32[4,4096]{1,0:T(4,128)S(1)} %copy.38) | copy-start | bytes 196612
  145.8 174.2 %copy-start.1 = (bf16[512,512]{1,0:T(8,128)(2,1)S(1)}, bf16[512,512]{1,0:T(8,128)(2,1)}, u32[]{:S(2)}) copy-start(bf16[512,512]{1,0:T(8,128)(2,1)} %param.8) | copy-start | bytes 1572868
Sparse Core Ops, SparseCore 0:
  164.1 154.0 all-reduce.1
where the time goes:
time: 327 us
  blocking collectives  132 us (40%)
  matrix products  57.4 us (18%)
  other arithmetic  51.9 us (16%)
  local copies, waits for them, and re-layouts  34.3 us (10%)
  waiting for transfers between devices  25.6 us (8%)
  between operations  14.3 us (4%)
  starting transfers between devices  11.1 us (3%)
    psum x1, blocking collectives, on_device(): lax.psum(loss_local, 'grid') / (patch_total * tiles * sharpness)  67.4 us
    psum x1, blocking collectives, on_device(): lax.psum((weight_term, vector_term), ('dp', 'grid'))  64.7 us
    dot_general x1, matrix products, on_device(): jnp.dot(flat_rows, weight_in, preferred_element_type=jnp.float32) + bias_in  29.1 us
    reduce_sum x1, other arithmetic, on_device(): bias_term = jnp.sum(epilogue.astype(jnp.float32), axis=0)  28 us
    psum x1, waiting for transfers between devices, on_device(): lax.psum((weight_term, vector_term), ('dp', 'grid'))  21.5 us
    dot_general x1, matrix products, on_device(): lax.dot_general(flat_rows, epilogue, (((0,), (0,)), ((), ())), preferred_...  18.1 us
    gather x1, local copies, waits for them, and re-layouts, on_device(): sorted_entries = jnp.take(prediction_residual, zorder_line, axis=1)  12.4 us
    reduce_sum x6, other arithmetic, on_device(): means = jnp.sum(grouped, axis=2) / node_cells  11.9 us
  transfers between devices with their start and end apart: 6, of which 5 were waited for; matrix products, arithmetic and copies ran while one was open for 5% of the time, Pallas kernels for 0%

commit v1 on v0

--- a/solution.py
+++ b/solution.py
@@ -79,7 +79,7 @@
     weight_term = grad_scale * lax.dot_general(
         flat_rows, epilogue, (((0,), (0,)), ((), ())), preferred_element_type=jnp.float32
     )
-    summed, offset_projection_derivs = lax.psum((weight_term, vector_term), ("dp", "grid"))
+    summed, offset_projection_derivs = lax.psum(lax.psum((weight_term, vector_term), "grid"), "dp")
     inner_coefficient_deriv = lax.dynamic_slice_in_dim(
         summed, lax.axis_index("grid") * kept, kept, 0
     )

time: 327 us -> 363 us (1.11); the launches traced: 327 us -> 357 us
  waiting for transfers between devices: 25.6 us -> 116 us
  blocking collectives: 132 us -> 72.6 us
    psum x1 -> x2, waiting for transfers between devices: 21.5 us -> 111 us  [the longest x1 111 us: on_device(): lax.psum((weight_term, vector_term), 'grid')]
    psum x1, blocking collectives: 64.7 us -> 9.05 us  [on_device(): lax.psum(lax.psum((weight_term, vector_term), 'grid'), 'dp')]
    psum x1, blocking collectives: 67.4 us -> 63.6 us  [on_device(): lax.psum(loss_local, 'grid') / (patch_total * tiles * sharpness)]
  transfers between devices with their start and end apart: 6 -> 7, of which waited for: 5 -> 5; matrix products, arithmetic and copies ran while one was open for 5% -> 4% of each run, Pallas kernels for 0% -> 0%
where the time goes in v1:
time: 363 us; the launch traced here: 357 us
  waiting for transfers between devices  116 us (32%)
  blocking collectives  72.6 us (20%)
  matrix products  57.4 us (16%)
  other arithmetic  51.9 us (14%)
  local copies, waits for them, and re-layouts  34.3 us (9%)
  between operations  14.3 us (4%)
  starting transfers between devices  11.1 us (3%)
    psum x1, waiting for transfers between devices, on_device(): lax.psum((weight_term, vector_term), 'grid')  111 us
    psum x1, blocking collectives, on_device(): lax.psum(loss_local, 'grid') / (patch_total * tiles * sharpness)  63.6 us
    dot_general x1, matrix products, on_device(): jnp.dot(flat_rows, weight_in, preferred_element_type=jnp.float32) + bias_in  29.1 us
    reduce_sum x1, other arithmetic, on_device(): bias_term = jnp.sum(epilogue.astype(jnp.float32), axis=0)  28 us
    dot_general x1, matrix products, on_device(): lax.dot_general(flat_rows, epilogue, (((0,), (0,)), ((), ())), preferred_...  18.1 us
    gather x1, local copies, waits for them, and re-layouts, on_device(): sorted_entries = jnp.take(prediction_residual, zorder_line, axis=1)  12.4 us
    reduce_sum x6, other arithmetic, on_device(): means = jnp.sum(grouped, axis=2) / node_cells  11.9 us
    scatter x1, local copies, waits for them, and re-layouts, on_device(): jnp.zeros_like(steepness).at[:, zorder_line].set(steepness)  11.8 us
  transfers between devices with their start and end apart: 7, of which 5 were waited for; matrix products, arithmetic and copies ran while one was open for 4% of the time, Pallas kernels for 0%

profile of v1, /device:TPU:1, one launch (start us, length us, event | category | flops | bytes accessed | tf_op | source)
XLA Modules:
  0.0 357.3 jit_solution(9199717303569504051)
XLA Ops:
  8.2 29.1 %multiply_convert_fusion.1 = (bf16[16384,512]{1,0:T(8,128)(2,1)}, f32[16384,512]{1,0:T(8,128)}) fusion(f32[512]{0:T(512)} %param.9, bf16[16384,512]{1,0:T(8,128)(2,1)} %bitcast.84, bf16[512,512]{1,0:T(8,128)(2,1)S(1)} %copy-done), kind=kOutput, calls=%fused_computation.5 | convolution fusion | flops 8640266240 | bytes 67635200 | tf_op jit(solution)/shard_map/dot_general | solution.py:34
  37.3 10.2 %fusion.14 = f32[1,16384]{1,0:T(1,128)S(1)} fusion(bf16[16384,512]{1,0:T(8,128)(2,1)} %get-tuple-element.45, bf16[512,1]{0,1:T(2,128)(2,1)S(1)} %reshape.178), kind=kOutput, calls=%fused_computation.73 | convolution fusion | flops 16777216 | bytes 16843776 | tf_op jit(solution)/shard_map/dot_general | solution.py:37
  48.4 2.0 copy.30
  50.4 2.9 subtract_multiply_fusion
  53.3 12.4 %gather_fusion = f32[4096,4]{1,0:T(8,128)S(1)} fusion(f32[4,4096]{0,1:T(8,128)} %subtract_multiply_fusion, s32[4096]{0:T(1024)S(1)} %broadcast_clamp_fusion), kind=kCustom, calls=%fused_computation | custom fusion | bytes 147456 | tf_op jit(solution)/shard_map/jit(_take)/gather | solution.py:43
  65.7 2.3 add_reduce_fusion
  67.9 1.6 collective-permute-start
  69.8 2.2 fusion
  73.8 5.9 %select_reduce_fusion.4 = f32[4,1024]{0,1:T(8,128)S(1)} fusion(f32[4,1024,4]{0,2,1:T(4,128)S(1)} %bitcast.70, pred[1024,4]{1,0:T(8,128)(4,1)S(1)} %compare_and_fusion), kind=kLoop, calls=%fused_computation.23 | loop fusion | flops 28672 | bytes 86016 | tf_op jit(solution)/shard_map/reduce_sum | solution.py:49
  82.9 1.6 select_reduce_fusion.3
  85.0 1.4 collective-permute-start.1
  86.4 1.1 collective-permute-done.1
  87.5 2.9 collective-permute-start.2
  91.4 1.8 collective-permute-start.3
  94.1 3.4 collective-permute-start.4
  98.9 3.0 fusion.4
  101.9 11.8 %scatter_custom_fusion = f32[4,4096]{0,1:T(8,128)S(1)} fusion(s32[4096]{0:T(1024)S(1)} %bitcast.81, f32[4,4096]{0,1:T(8,128)} %fusion.4, f32[]{:T(128)} %constant.37.clone.1), kind=kCustom, calls=%fused_computation.9 | custom fusion | bytes 131076 | tf_op jit(solution)/shard_map/scatter | solution.py:67
  113.7 1.9 broadcast_multiply_fusion
  115.6 2.2 copy.38
  117.8 28.0 %convert_reduce_fusion = (f32[512]{0:T(512)S(1)}, bf16[16384,512]{1,0:T(8,128)(2,1)}, f32[512]{0:T(512)S(1)}) fusion(f32[16384,512]{1,0:T(8,128)} %get-tuple-element.46, f32[512]{0:T(512)S(1)} %copy-done.8, f32[512]{0:T(512)S(1)} %convert_element_type.20, f32[16384]{0:T(1024)S(1)} %bitcast.78, bf16[16384,512]{1,0:T(8,128)(2,1)} %get-tuple-element.45), kind=kLoop, calls=%fused_computation.3 | loop fusion | flops 134216704 | bytes 67182592 | tf_op jit(solution)/shard_map/reduce_sum | solution.py:75
  145.8 18.1 %fusion.7 = f32[512,512]{0,1:T(8,128)} fusion(bf16[16384,512]{1,0:T(8,128)(2,1)} %get-tuple-element.30, bf16[16384,512]{1,0:T(8,128)(2,1)} %bitcast.85), kind=kOutput, calls=%fused_computation.30 | convolution fusion | flops 8590196736 | bytes 34603008 | tf_op jit(solution)/shard_map/dot_general | solution.py:79
  164.0 111.4 %all-reduce.4.cloned.1.call-done = f32[512,512]{0,1:T(8,128)} async-done(((f32[512,512]{0,1:T(8,128)}), f32[512,512]{0,1:T(8,128)}) %all-reduce.4.cloned.1.call-update) | async-done | bytes 1048592 | tf_op jit(solution)/shard_map/psum | solution.py:82
  275.5 63.6 %all-reduce = (f32[4]{0:T(128)S(1)}, f32[2,512]{1,0:T(2,128)S(1)}) all-reduce(f32[4]{0:T(128)S(1)} %get-tuple-element.42, f32[2,512]{1,0:T(2,128)S(1)} %maximum_multiply_fusion), channel_id=1, replica_groups=mesh['dp'=4,'grid'=32] {'grid'}, use_global_device_ids=true, to_apply=%region_14.15 | all-reduce | flops 1028 | bytes 8224 | tf_op jit(solution)/shard_map/psum | solution.py:65
  339.1 9.0 %psum.39 = f32[2,512]{1,0:T(2,128)} all-reduce(f32[2,512]{1,0:T(2,128)S(1)} %get-tuple-element.28), channel_id=1, replica_groups=mesh['dp'=4,'grid'=32] {'dp'}, use_global_device_ids=true, to_apply=%region_20.21 | all-reduce | flops 1024 | bytes 8192 | tf_op jit(solution)/shard_map/psum | solution.py:82
  (72 shorter events, 13.3 us)
Async XLA Ops:
  7.2 1.1 copy-start
  7.2 268.2 %all-reduce.4.cloned.1.call-start = ((), (), s32[]{:S(2)}) async-start(), calls=%async_computation | async-start | bytes 2097152 | tf_op jit(solution)/shard_map/psum | solution.py:82
  37.3 10.2 %copy-start.2 = (s32[1,4096]{1,0:T(1,128)S(1)}, s32[1,4096]{1,0:T(1,128)}, u32[]{:S(2)}) copy-start(s32[1,4096]{1,0:T(1,128)} %param.13) | copy-start | bytes 49156
  47.5 0.9 copy-start.5
  47.6 2.8 copy-start.3
  47.6 2.7 copy-start.6
  65.7 6.3 %copy-start.7 = (bf16[512]{0:T(512)(128)(2,1)S(1)}, bf16[512]{0:T(512)(128)(2,1)}, u32[]{:S(2)}) copy-start(bf16[512]{0:T(512)(128)(2,1)} %param.10) | copy-start | bytes 3076
  67.9 17.0 %collective-permute-start = (f32[4]{0:T(128)S(1)}, f32[4]{0:T(128)S(1)}, u32[]{:S(2)}, u32[]{:S(2)}) collective-permute-start(f32[4]{0:T(128)S(1)} %get-tuple-element.26), channel_id=1, source_target_pairs={{0,1},{1,0},{2,3},{3,2},{4,5},{5,4},{6,7},{7,6},{8,9},{9,8},{10,11... | collective-permute-start | bytes 56 | tf_op jit(solution)/shard_map/ppermute | solution.py:16
  85.0 2.5 collective-permute-start.1
  87.5 3.9 %collective-permute-start.2 = (f32[4]{0:T(128)S(1)}, f32[4]{0:T(128)S(1)}, u32[]{:S(2)}, u32[]{:S(2)}) collective-permute-start(f32[4]{0:T(128)S(1)} %add.246), channel_id=1, source_target_pairs={{0,4},{4,0},{1,5},{5,1},{2,6},{6,2},{3,7},{7,3},{8,12},{12,8},{9,1... | collective-permute-start | bytes 56 | tf_op jit(solution)/shard_map/ppermute | solution.py:16
  91.4 2.7 collective-permute-start.3
  94.1 4.4 %collective-permute-start.4 = (f32[4]{0:T(128)S(1)}, f32[4]{0:T(128)S(1)}, u32[]{:S(2)}, u32[]{:S(2)}) collective-permute-start(f32[4]{0:T(128)S(1)} %add.249), channel_id=1, source_target_pairs={{0,16},{16,0},{1,17},{17,1},{2,18},{18,2},{3,19},{19,3},{4,20},{20... | collective-permute-start | bytes 56 | tf_op jit(solution)/shard_map/ppermute | solution.py:16
  115.6 2.2 copy-start.8
  117.8 28.0 %copy-start.4 = (f32[4,4096]{1,0:T(4,128)}, f32[4,4096]{1,0:T(4,128)S(1)}, u32[]{:S(2)}) copy-start(f32[4,4096]{1,0:T(4,128)S(1)} %copy.38) | copy-start | bytes 196612
  145.8 204.6 %copy-start.1 = (bf16[512,512]{1,0:T(8,128)(2,1)S(1)}, bf16[512,512]{1,0:T(8,128)(2,1)}, u32[]{:S(2)}) copy-start(bf16[512,512]{1,0:T(8,128)(2,1)} %param.8) | copy-start | bytes 1572868
  164.0 184.7 %all-reduce.6.cloned.1.call-start = ((), (), s32[]{:S(2)}) async-start(), calls=%async_computation.1 | async-start | bytes 2097152 | tf_op jit(solution)/shard_map/psum | solution.py:82
Sparse Core Ops, SparseCore 0:
  164.1 111.2 all-reduce.3
  277.8 43.7 all-reduce.5
